TPU v7x, 512 devices: a whole 4x4x16 slice. The times are simulated.
512 devices in a mesh: slab: 64 (over z_lo, x, core), grp: 8 (over z_hi, y).
Axes of the slice: x: 4, y: 4, z: 16 (z_hi: 2, z_lo: 8; z = z_hi * 8 + z_lo), core: 2. Of those that a mesh axis runs over, the one named last changes fastest.
Arguments:
- adj_out: float32 [5, 512, 256, 256], P(None, 'grp', 'slab'), may hold values from -6 to 6
- advect: bfloat16 [3, 512, 256, 256], P(None, 'grp', 'slab'), may hold values from -4 to 4
- viscosity: bfloat16 [512, 256, 256], P('grp', 'slab'), may hold values from 0.099609375 to 0.796875
- body_mask: int32 [512, 256, 256], P('grp', 'slab'), may hold values 0 or 1
- marker_x: int32 [2048], replicated, may hold values from 128 to 191
- marker_z: int32 [2048], replicated, may hold values from 0 to 255
- marker_y: int32 [2048], replicated, may hold values from 64 to 191
- drag_weight: float32 [2048], replicated, may hold values from -5 to 5
- inv_x: float32 [512, 512], P(None, 'grp'), may hold values from 0 to 1, as said below
- inv_y: float32 [256, 256], replicated, may hold values from 0 to 1, as said below
- inv_z: float32 [256, 256], replicated, may hold values from 0 to 1, as said below
Outputs:
- state_adjoint: float32 [5, 512, 256, 256], P(None, 'grp', 'slab')
Inputs may be any that keep to these rules, and one draw needn't show every extreme that they name: `inv_x`: entries of a given inverse. `inv_y`: entries of a given inverse. `inv_z`: entries of a given inverse.
All inputs are finite; a program needn't handle non-finite values. No bound on the sum of `body_mask` on one device may be relied on, other than what follows from the above.
Results may differ from a plain program's by a relative error of at most 0.0003.
Values sent between devices are 32-bit elements; how exact they have to be, the bound alone decides.
No kernel may reach another device: no remote copies, remote signals or barrier semaphores. Data moves between devices by JAX's collectives and lax.ppermute only.
A program may use at most 64 MiB of HBM per device.

v0:
```python
import jax
import jax.numpy as jnp
from jax import lax
from jax.sharding import PartitionSpec as P

time_step = 0.08
highest = lax.Precision.HIGHEST


def extended(cells, sides, width):
    for axis, dim in sides:
        count = lax.axis_size(axis)
        ends = count - 1
        head = lax.slice_in_dim(cells, 0, width, axis=dim)
        tail = lax.slice_in_dim(cells, cells.shape[dim] - width, cells.shape[dim], axis=dim)
        cells = jnp.concatenate(
            [
                lax.ppermute(tail, axis, [(i, (i + 1) % count) for i in range(ends)]),
                cells,
                lax.ppermute(head, axis, [((i + 1) % count, i) for i in range(ends)]),
            ],
            axis=dim,
        )
    return cells


def body(
    adj_out,
    advect,
    viscosity,
    body_mask,
    marker_x,
    marker_z,
    marker_y,
    drag_weight,
    inv_x,
    inv_y,
    inv_z,
):
    fields, x_rows, z_rows, y_cells = adj_out.shape
    x_offset = lax.axis_index("grp") * x_rows
    z_offset = lax.axis_index("slab") * z_rows
    local_x = marker_x - x_offset
    local_z = marker_z - z_offset
    inside = (local_x >= 0) & (local_x < x_rows) & (local_z >= 0) & (local_z < z_rows)
    flat_index = jnp.where(inside, (local_x * z_rows + local_z) * y_cells + marker_y, 0)
    pushed = jax.ops.segment_sum(
        jnp.where(inside, drag_weight, 0.0), flat_index, num_segments=x_rows * z_rows * y_cells
    )
    seeded = adj_out.at[0].add(pushed.reshape(x_rows, z_rows, y_cells))
    zlines = lax.all_to_all(seeded, "slab", split_axis=1, concat_axis=2, tiled=True)
    zlines = jnp.einsum("jk,cxjy->cxky", inv_z, zlines, precision=highest)
    zlines = jnp.einsum("jk,cxzj->cxzk", inv_y, zlines, precision=highest)
    returned = lax.all_to_all(zlines, "slab", split_axis=2, concat_axis=1, tiled=True)
    solved = jnp.einsum(
        "jk,cjzy->ckzy",
        inv_x,
        lax.all_gather(returned, "grp", axis=1, tiled=True),
        precision=highest,
    )
    masked = solved * body_mask.astype(jnp.float32)
    rimmed = extended(masked, (("slab", 2), ("grp", 1)), 1)
    centre = rimmed[:, 1:-1, 1:-1, :]
    y_padded = jnp.pad(centre, ((0, 0), (0, 0), (0, 0), (1, 1)))
    grad_x = (rimmed[:, 2:, 1:-1, :] - rimmed[:, :-2, 1:-1, :]) * 0.5
    grad_z = (rimmed[:, 1:-1, 2:, :] - rimmed[:, 1:-1, :-2, :]) * 0.5
    grad_y = (y_padded[..., 2:] - y_padded[..., :-2]) * 0.5
    laplace = (
        rimmed[:, 2:, 1:-1, :]
        + rimmed[:, :-2, 1:-1, :]
        + rimmed[:, 1:-1, 2:, :]
        + rimmed[:, 1:-1, :-2, :]
        + y_padded[..., 2:]
        + y_padded[..., :-2]
        - 6.0 * centre
    )
    velocity = advect.astype(jnp.float32)
    viscous = viscosity.astype(jnp.float32)
    change = velocity[0] * grad_x + velocity[1] * grad_z + velocity[2] * grad_y + viscous * laplace
    return centre + time_step * change


def solution(mesh):
    in_specs = (
        P(None, "grp", "slab", None),
        P(None, "grp", "slab", None),
        P("grp", "slab", None),
        P("grp", "slab", None),
        P(),
        P(),
        P(),
        P(),
        P(None, "grp"),
        P(),
        P(),
    )
    out_specs = P(None, "grp", "slab", None)
    return jax.shard_map(body, mesh=mesh, in_specs=in_specs, out_specs=out_specs, check_vma=False)
```

profile of v0, /device:TPU:352, one launch (start us, length us, event | category | flops | bytes accessed | tf_op | source)
XLA Modules:
  0.0 591.5 jit_solution(2021794597790402186)
XLA Ops:
  6.5 0.0 copy-start
  6.5 0.0 all-gather.2.cloned.1.call-start
  6.5 0.8 add_select_fusion
  7.3 0.7 broadcast_select_fusion
  8.1 14.8 %scatter_custom_fusion = f32[65536]{0:T(1024)S(1)} fusion(s32[2048]{0:T(1024)S(1)} %add_select_fusion, f32[2048]{0:T(1024)S(1)} %broadcast_select_fusion, f32[]{:T(128)} %constant.45.clone.1), kind=kCustom, calls=%fused_computation.27 | custom fusion | flops 2048 | bytes 262148 | tf_op jit(solution)/shard_map/scatter-add | solution.py:47
  22.8 0.1 reshape.62
  23.0 1.5 copy.57
  24.5 0.1 fusion.4
  24.6 68.9 %all_to_all.21 = f32[5,64,4,256]{3,2,0,1:T(4,128)S(1)} all-to-all(f32[5,64,4,256]{3,2,0,1:T(4,128)S(1)} %fusion.4), channel_id=1, replica_groups=mesh['slab'=64,'grp'=8] {'slab'}, dimensions={1} | all-to-all | bytes 2621440 | tf_op jit(solution)/shard_map/all_to_all | solution.py:51
  93.5 0.2 copy.58
  93.8 0.5 reshape.63
  94.2 0.0 copy-done
  94.2 0.0 copy-start.3
  94.3 2.2 convolution_bitcast_fusion.1
  96.5 0.0 copy-done.3
  96.5 2.3 convolution_bitcast_fusion
  98.8 1.3 copy.61
  100.1 70.3 %all_to_all.22 = f32[5,1,256,256]{3,1,0,2:T(1,128)S(1)} all-to-all(f32[5,1,256,256]{3,1,0,2:T(1,128)S(1)} %copy.61), channel_id=1, replica_groups=mesh['slab'=64,'grp'=8] {'slab'}, dimensions={2} | all-to-all | bytes 2621440 | tf_op jit(solution)/shard_map/all_to_all | solution.py:54
  170.4 0.3 copy.75
  170.7 1.8 copy.63
  172.5 0.0 copy-start.2
  172.5 0.0 copy-start.4
  172.5 0.0 all-gather.2.cloned.1.call-update
  172.5 0.9 copy-done.2
  173.5 0.1 copy.64
  173.6 324.0 %all-gather.2.cloned.1.call-done = f32[5,512,4,256]{3,1,2,0:T(8,128)} async-done(((f32[5,64,4,256]{3,1,2,0:T(8,128)}), f32[5,512,4,256]{3,1,2,0:T(8,128)}) %all-gather.2.cloned.1.call-update) | async-done | bytes 10485776 | tf_op jit(solution)/shard_map/all_gather | solution.py:58
  497.6 0.0 copy-done.4
  497.6 9.5 %fusion = f32[5,64,4,256]{3,1,2,0:T(8,128)S(1)} fusion(f32[5,512,4,256]{3,1,2,0:T(8,128)} %all-gather.2.cloned.1.call-done, f32[64,4,256]{2,0,1:T(8,128)S(1)} %copy.64, f32[512,64]{0,1:T(8,128)S(1)} %copy-done.4), kind=kOutput, calls=%fused_computation.6 | convolution fusion | flops 2013593600 | bytes 12189696 | tf_op jit(solution)/shard_map/jk,cjzy->ckzy/dot_general | solution.py:55
  507.1 0.0 copy-start.1
  507.2 0.1 fusion.10
  507.2 2.1 collective-permute-start
  509.3 38.0 %collective-permute-start.1 = (f32[5,64,1,256]{3,1,2,0:T(8,128)S(1)}, f32[5,64,1,256]{3,1,2,0:T(8,128)S(1)}, u32[]{:S(2)}, u32[]{:S(2)}) collective-permute-start(f32[5,64,1,256]{3,1,2,0:T(8,128)S(1)} %get-tuple-element.20), channel_id=1, source_target_pairs={{8,0},{16,8},{24,16},{32,24},{40,32},{48,40},{56,48},{64,56},{72,6... | collective-permute-start | bytes 983048 | tf_op jit(solution)/shard_map/ppermute | solution.py:20
  547.3 0.0 copy-done.1
  547.3 0.1 convert_element_type.12
  547.5 2.7 collective-permute-done
  550.1 2.1 collective-permute-done.1
  552.3 11.7 %collective-permute-start.2 = (f32[5,1,6,256]{3,1,2,0:T(1,128)S(1)}, f32[5,1,6,256]{3,1,2,0:T(1,128)S(1)}, u32[]{:S(2)}, u32[]{:S(2)}) collective-permute-start(f32[5,1,6,256]{3,1,2,0:T(1,128)S(1)} %get-tuple-element.18), channel_id=1, source_target_pairs={{1,0},{2,1},{3,2},{4,3},{5,4},{6,5},{7,6},{9,8},{10,9},{11,10},{12... | collective-permute-start | bytes 92168 | tf_op jit(solution)/shard_map/ppermute | solution.py:20
  564.0 0.0 copy-start.5
  564.0 2.1 collective-permute-start.3
  566.1 0.2 fusion.3
  566.3 0.1 copy.65
  566.3 0.1 copy.66
  566.4 0.1 copy.67
  566.4 0.0 copy-done.5
  566.5 0.0 collective-permute-done.2
  566.5 14.3 %collective-permute-done.3 = f32[5,1,6,256]{3,1,2,0:T(1,128)S(1)} collective-permute-done((f32[5,1,6,256]{3,1,2,0:T(1,128)S(1)}, f32[5,1,6,256]{3,1,2,0:T(1,128)S(1)}, u32[]{:S(2)}, u32[]{:S(2)}) %collective-permute-start.3) | collective-permute-done | bytes 30752 | tf_op jit(solution)/shard_map/ppermute | solution.py:18
  580.7 2.0 multiply_add_fusion
  582.8 1.9 copy.69
  (3 shorter events, 0.1 us)
Async XLA Ops:
  6.5 87.7 %copy-start = (f32[256,256]{1,0:T(8,128)S(1)}, f32[256,256]{1,0:T(8,128)}, u32[]{:S(2)}) copy-start(f32[256,256]{1,0:T(8,128)} %param.23) | copy-start | bytes 786436
  6.5 491.1 %all-gather.2.cloned.1.call-start = ((), (), s32[]{:S(2)}) async-start(), calls=%async_computation.2 | async-start | bytes 11796480 | tf_op jit(solution)/shard_map/all_gather | solution.py:58
  94.2 2.2 copy-start.3
  172.5 0.9 copy-start.2
  172.5 325.1 %copy-start.4 = (f32[512,64]{0,1:T(8,128)S(1)}, f32[512,64]{0,1:T(8,128)}, u32[]{:S(2)}) copy-start(f32[512,64]{0,1:T(8,128)} %param.21) | copy-start | bytes 393220
  507.1 40.2 %copy-start.1 = (bf16[3,64,4,256]{3,2,1,0:T(4,128)(2,1)S(1)}, bf16[3,64,4,256]{3,2,1,0:T(4,128)(2,1)}, u32[]{:S(2)}) copy-start(bf16[3,64,4,256]{3,2,1,0:T(4,128)(2,1)} %param.14) | copy-start | bytes 1179652
  507.2 42.9 %collective-permute-start = (f32[5,64,1,256]{3,1,2,0:T(8,128)S(1)}, f32[5,64,1,256]{3,1,2,0:T(8,128)S(1)}, u32[]{:S(2)}, u32[]{:S(2)}) collective-permute-start(f32[5,64,1,256]{3,1,2,0:T(8,128)S(1)} %get-tuple-element.19), channel_id=1, source_target_pairs={{0,8},{8,16},{16,24},{24,32},{32,40},{40,48},{48,56},{56,64},{64,7... | collective-permute-start | bytes 983048 | tf_op jit(solution)/shard_map/ppermute | solution.py:18
  509.3 42.9 %collective-permute-start.1 = (f32[5,64,1,256]{3,1,2,0:T(8,128)S(1)}, f32[5,64,1,256]{3,1,2,0:T(8,128)S(1)}, u32[]{:S(2)}, u32[]{:S(2)}) collective-permute-start(f32[5,64,1,256]{3,1,2,0:T(8,128)S(1)} %get-tuple-element.20), channel_id=1, source_target_pairs={{8,0},{16,8},{24,16},{32,24},{40,32},{48,40},{56,48},{64,56},{72,6... | collective-permute-start | bytes 983048 | tf_op jit(solution)/shard_map/ppermute | solution.py:20
  552.3 14.2 %collective-permute-start.2 = (f32[5,1,6,256]{3,1,2,0:T(1,128)S(1)}, f32[5,1,6,256]{3,1,2,0:T(1,128)S(1)}, u32[]{:S(2)}, u32[]{:S(2)}) collective-permute-start(f32[5,1,6,256]{3,1,2,0:T(1,128)S(1)} %get-tuple-element.18), channel_id=1, source_target_pairs={{1,0},{2,1},{3,2},{4,3},{5,4},{6,5},{7,6},{9,8},{10,9},{11,10},{12... | collective-permute-start | bytes 92168 | tf_op jit(solution)/shard_map/ppermute | solution.py:20
  564.0 2.5 copy-start.5
  564.0 16.7 %collective-permute-start.3 = (f32[5,1,6,256]{3,1,2,0:T(1,128)S(1)}, f32[5,1,6,256]{3,1,2,0:T(1,128)S(1)}, u32[]{:S(2)}, u32[]{:S(2)}) collective-permute-start(f32[5,1,6,256]{3,1,2,0:T(1,128)S(1)} %get-tuple-element.17), channel_id=1, source_target_pairs={{0,1},{1,2},{2,3},{3,4},{4,5},{5,6},{6,7},{8,9},{9,10},{10,11},{11... | collective-permute-start | bytes 92168 | tf_op jit(solution)/shard_map/ppermute | solution.py:18
Sparse Core Ops, SparseCore 0:
  172.7 324.8 all-gather.1
where the time goes:
time: 592 us
  waiting for transfers between devices  343 us (58%)
  blocking collectives  139 us (23%)
  starting transfers between devices  53.8 us (9%)
  other arithmetic  18.8 us (3%)
  matrix products  14 us (2%)
  between operations  13.6 us (2%)
  local copies, waits for them, and re-layouts  8.92 us (2%)
    all_gather x1, waiting for transfers between devices, body(): lax.all_gather(returned, 'grp', axis=1, tiled=True)  324 us
    all_to_all x1, blocking collectives, body(): lax.all_to_all(zlines, 'slab', split_axis=2, concat_axis=1, tiled=True)  70.3 us
    all_to_all x1, blocking collectives, body(): lax.all_to_all(seeded, 'slab', split_axis=1, concat_axis=2, tiled=True)  68.9 us
    ppermute x2, starting transfers between devices, extended(): lax.ppermute(head, axis, [((i + 1) % count, i) for i in range(ends)])  49.7 us
    ppermute x2, waiting for transfers between devices, extended(): lax.ppermute(tail, axis, [(i, (i + 1) % count) for i in range(ends)])  17 us
    scatter-add x1, other arithmetic, body(): jax.ops.segment_sum(jnp.where(inside, drag_weight, 0.0), flat_index, num_...  14.8 us
  transfers between devices with their start and end apart: 5, of which 4 were waited for; matrix products, arithmetic and copies ran while one was open for 0% of the time, Pallas kernels for 0%

commit v1 on v0

--- a/solution.py
+++ b/solution.py
@@ -48,7 +48,10 @@
         jnp.where(inside, drag_weight, 0.0), flat_index, num_segments=x_rows * z_rows * y_cells
     )
     seeded = adj_out.at[0].add(pushed.reshape(x_rows, z_rows, y_cells))
-    zlines = lax.all_to_all(seeded, "slab", split_axis=1, concat_axis=2, tiled=True)
+    zlines = jnp.concatenate(
+        lax.all_to_all(jnp.stack(jnp.split(seeded, lax.axis_size("slab"), axis=1)), "slab", 0, 0),
+        axis=2,
+    )
     zlines = jnp.einsum("jk,cxjy->cxky", inv_z, zlines, precision=highest)
     zlines = jnp.einsum("jk,cxzj->cxzk", inv_y, zlines, precision=highest)
     returned = lax.all_to_all(zlines, "slab", split_axis=2, concat_axis=1, tiled=True)

time: 592 us -> 591 us (level)
  no operation moved by 1% of the time
where the time goes in v1:
time: 591 us; the launch traced here: 590 us
  waiting for transfers between devices  343 us (58%)
  blocking collectives  139 us (24%)
  starting transfers between devices  53.9 us (9%)
  other arithmetic  17.3 us (3%)
  matrix products  14 us (2%)
  between operations  14 us (2%)
  local copies, waits for them, and re-layouts  8.87 us (2%)
    all_gather x1, waiting for transfers between devices, body(): lax.all_gather(returned, 'grp', axis=1, tiled=True)  324 us
    all_to_all x1, blocking collectives, body(): lax.all_to_all(zlines, 'slab', split_axis=2, concat_axis=1, tiled=True)  70.3 us
    all_to_all x1, blocking collectives, body(): lax.all_to_all(jnp.stack(jnp.split(seeded, lax.axis_size('slab'), axis=1)...  68.9 us
    ppermute x2, starting transfers between devices, extended(): lax.ppermute(head, axis, [((i + 1) % count, i) for i in range(ends)])  49.7 us
    ppermute x2, waiting for transfers between devices, extended(): lax.ppermute(tail, axis, [(i, (i + 1) % count) for i in range(ends)])  17 us
    scatter-add x1, other arithmetic, body(): jax.ops.segment_sum(jnp.where(inside, drag_weight, 0.0), flat_index, num_...  14.8 us
  transfers between devices with their start and end apart: 5, of which 4 were waited for; matrix products, arithmetic and copies ran while one was open for 0% of the time, Pallas kernels for 0%

profile of v1, /device:TPU:352, one launch (start us, length us, event | category | flops | bytes accessed | tf_op | source)
XLA Modules:
  0.0 590.4 jit_solution(14619964165415629873)
XLA Ops:
  6.5 0.0 copy-start
  6.5 0.0 copy-start.10
  6.6 0.0 all-gather.2.cloned.1.call-start
  6.6 0.7 copy-done.8
  7.4 0.0 copy-done.7
  7.4 0.0 copy-done.9
  7.4 0.0 copy-done.10
  7.4 14.8 %scatter_custom_fusion = f32[65536]{0:T(1024)S(1)} fusion(s32[2048]{0:T(1024)S(1)} %add_select_fusion, f32[2048]{0:T(1024)S(1)} %broadcast_select_fusion, f32[]{:T(128)} %constant.45.clone.1), kind=kCustom, calls=%fused_computation.90 | custom fusion | flops 2048 | bytes 262148 | tf_op jit(solution)/shard_map/scatter-add | solution.py:47
  22.2 0.1 reshape.63
  22.3 0.0 copy-done.1
  22.3 0.1 add_dynamic-update-slice_fusion
  23.5 68.9 %all_to_all.17 = f32[64,5,1,4,256]{4,3,1,2,0:T(4,128)S(1)} all-to-all(f32[64,5,1,4,256]{4,3,1,2,0:T(4,128)S(1)} %constant_dynamic-update-slice_fusion), channel_id=1, replica_groups=mesh['slab'=64,'grp'=8] {'slab'}, dimensions={0} | all-to-all | bytes 2621440 | tf_op jit(solution)/shard_map/all_to_all | solution.py:52
  92.4 0.2 copy.368
  92.6 0.5 reshape.65
  93.1 0.0 copy-done
  93.1 0.0 copy-start.4
  93.1 2.2 convolution_bitcast_fusion.1
  95.3 0.0 copy-done.4
  95.4 2.3 convolution_bitcast_fusion
  97.6 1.3 copy.371
  99.0 70.3 %all_to_all.18 = f32[5,1,256,256]{3,1,0,2:T(1,128)S(1)} all-to-all(f32[5,1,256,256]{3,1,0,2:T(1,128)S(1)} %copy.371), channel_id=1, replica_groups=mesh['slab'=64,'grp'=8] {'slab'}, dimensions={2} | all-to-all | bytes 2621440 | tf_op jit(solution)/shard_map/all_to_all | solution.py:57
  169.3 0.3 copy.385
  169.6 1.8 copy.373
  171.4 0.0 all-gather.2.cloned.1.call-update
  171.4 0.9 copy-done.3
  172.4 0.1 copy.374
  172.4 324.0 %all-gather.2.cloned.1.call-done = f32[5,512,4,256]{3,1,2,0:T(8,128)} async-done(((f32[5,64,4,256]{3,1,2,0:T(8,128)}), f32[5,512,4,256]{3,1,2,0:T(8,128)}) %all-gather.2.cloned.1.call-update) | async-done | bytes 10485776 | tf_op jit(solution)/shard_map/all_gather | solution.py:61
  496.5 0.0 copy-done.5
  496.5 9.6 %fusion = f32[5,64,4,256]{3,1,2,0:T(8,128)S(1)} fusion(f32[5,512,4,256]{3,1,2,0:T(8,128)} %all-gather.2.cloned.1.call-done, f32[64,4,256]{2,0,1:T(8,128)S(1)} %copy.374, f32[512,64]{0,1:T(8,128)S(1)} %copy-done.5), kind=kOutput, calls=%fused_computation.6 | convolution fusion | flops 2013593600 | bytes 12189696 | tf_op jit(solution)/shard_map/jk,cjzy->ckzy/dot_general | solution.py:58
  506.0 0.0 copy-start.2
  506.0 0.1 fusion.9
  506.1 2.1 collective-permute-start
  508.1 38.0 %collective-permute-start.1 = (f32[5,64,1,256]{3,1,2,0:T(8,128)S(1)}, f32[5,64,1,256]{3,1,2,0:T(8,128)S(1)}, u32[]{:S(2)}, u32[]{:S(2)}) collective-permute-start(f32[5,64,1,256]{3,1,2,0:T(8,128)S(1)} %get-tuple-element.20), channel_id=1, source_target_pairs={{8,0},{16,8},{24,16},{32,24},{40,32},{48,40},{56,48},{64,56},{72,6... | collective-permute-start | bytes 983048 | tf_op jit(solution)/shard_map/ppermute | solution.py:20
  546.2 0.1 convert_element_type.12
  546.3 2.7 collective-permute-done
  549.0 2.1 collective-permute-done.1
  551.1 11.7 %collective-permute-start.2 = (f32[5,1,6,256]{3,1,2,0:T(1,128)S(1)}, f32[5,1,6,256]{3,1,2,0:T(1,128)S(1)}, u32[]{:S(2)}, u32[]{:S(2)}) collective-permute-start(f32[5,1,6,256]{3,1,2,0:T(1,128)S(1)} %get-tuple-element.18), channel_id=1, source_target_pairs={{1,0},{2,1},{3,2},{4,3},{5,4},{6,5},{7,6},{9,8},{10,9},{11,10},{12... | collective-permute-start | bytes 92168 | tf_op jit(solution)/shard_map/ppermute | solution.py:20
  562.9 0.0 copy-start.6
  562.9 2.1 collective-permute-start.3
  564.9 0.2 fusion.3
  565.1 0.1 copy.375
  565.2 0.1 copy.376
  565.2 0.1 copy.377
  565.3 0.0 copy-done.6
  565.3 0.0 collective-permute-done.2
  565.3 14.3 %collective-permute-done.3 = f32[5,1,6,256]{3,1,2,0:T(1,128)S(1)} collective-permute-done((f32[5,1,6,256]{3,1,2,0:T(1,128)S(1)}, f32[5,1,6,256]{3,1,2,0:T(1,128)S(1)}, u32[]{:S(2)}, u32[]{:S(2)}) %collective-permute-start.3) | collective-permute-done | bytes 30752 | tf_op jit(solution)/shard_map/ppermute | solution.py:18
  579.6 2.0 multiply_add_fusion
  581.6 1.9 copy.379
  (76 shorter events, 0.8 us)
Async XLA Ops:
  6.5 86.6 %copy-start = (f32[256,256]{1,0:T(8,128)S(1)}, f32[256,256]{1,0:T(8,128)}, u32[]{:S(2)}) copy-start(f32[256,256]{1,0:T(8,128)} %param.23) | copy-start | bytes 786436
  6.5 15.8 %copy-start.1 = (f32[5,64,4,256]{3,2,1,0:T(4,128)S(1)}, f32[5,64,4,256]{3,2,1,0:T(4,128)}, u32[]{:S(2)}) copy-start(f32[5,64,4,256]{3,2,1,0:T(4,128)} %param.13) | copy-start | bytes 3932164
  6.5 0.8 copy-start.8
  6.5 0.8 copy-start.7
  6.5 0.8 copy-start.9
  6.5 0.9 copy-start.10
  6.6 489.9 %all-gather.2.cloned.1.call-start = ((), (), s32[]{:S(2)}) async-start(), calls=%async_computation.2 | async-start | bytes 11796480 | tf_op jit(solution)/shard_map/all_gather | solution.py:61
  93.1 2.2 copy-start.4
  171.4 0.9 copy-start.3
  171.4 325.1 %copy-start.5 = (f32[512,64]{0,1:T(8,128)S(1)}, f32[512,64]{0,1:T(8,128)}, u32[]{:S(2)}) copy-start(f32[512,64]{0,1:T(8,128)} %param.21) | copy-start | bytes 393220
  506.0 40.2 %copy-start.2 = (bf16[3,64,4,256]{3,2,1,0:T(4,128)(2,1)S(1)}, bf16[3,64,4,256]{3,2,1,0:T(4,128)(2,1)}, u32[]{:S(2)}) copy-start(bf16[3,64,4,256]{3,2,1,0:T(4,128)(2,1)} %param.14) | copy-start | bytes 1179652
  506.1 42.9 %collective-permute-start = (f32[5,64,1,256]{3,1,2,0:T(8,128)S(1)}, f32[5,64,1,256]{3,1,2,0:T(8,128)S(1)}, u32[]{:S(2)}, u32[]{:S(2)}) collective-permute-start(f32[5,64,1,256]{3,1,2,0:T(8,128)S(1)} %get-tuple-element.19), channel_id=1, source_target_pairs={{0,8},{8,16},{16,24},{24,32},{32,40},{40,48},{48,56},{56,64},{64,7... | collective-permute-start | bytes 983048 | tf_op jit(solution)/shard_map/ppermute | solution.py:18
  508.1 42.9 %collective-permute-start.1 = (f32[5,64,1,256]{3,1,2,0:T(8,128)S(1)}, f32[5,64,1,256]{3,1,2,0:T(8,128)S(1)}, u32[]{:S(2)}, u32[]{:S(2)}) collective-permute-start(f32[5,64,1,256]{3,1,2,0:T(8,128)S(1)} %get-tuple-element.20), channel_id=1, source_target_pairs={{8,0},{16,8},{24,16},{32,24},{40,32},{48,40},{56,48},{64,56},{72,6... | collective-permute-start | bytes 983048 | tf_op jit(solution)/shard_map/ppermute | solution.py:20
  551.1 14.2 %collective-permute-start.2 = (f32[5,1,6,256]{3,1,2,0:T(1,128)S(1)}, f32[5,1,6,256]{3,1,2,0:T(1,128)S(1)}, u32[]{:S(2)}, u32[]{:S(2)}) collective-permute-start(f32[5,1,6,256]{3,1,2,0:T(1,128)S(1)} %get-tuple-element.18), channel_id=1, source_target_pairs={{1,0},{2,1},{3,2},{4,3},{5,4},{6,5},{7,6},{9,8},{10,9},{11,10},{12... | collective-permute-start | bytes 92168 | tf_op jit(solution)/shard_map/ppermute | solution.py:20
  562.9 2.5 copy-start.6
  562.9 16.7 %collective-permute-start.3 = (f32[5,1,6,256]{3,1,2,0:T(1,128)S(1)}, f32[5,1,6,256]{3,1,2,0:T(1,128)S(1)}, u32[]{:S(2)}, u32[]{:S(2)}) collective-permute-start(f32[5,1,6,256]{3,1,2,0:T(1,128)S(1)} %get-tuple-element.17), channel_id=1, source_target_pairs={{0,1},{1,2},{2,3},{3,4},{4,5},{5,6},{6,7},{8,9},{9,10},{10,11},{11... | collective-permute-start | bytes 92168 | tf_op jit(solution)/shard_map/ppermute | solution.py:18
Sparse Core Ops, SparseCore 0:
  171.5 324.8 all-gather.1
